TPU v7x, 512 devices: a whole 4x4x16 slice. The times are simulated.
512 devices in a mesh: dp: 4 (over y), frames: 16 (over z), height: 8 (over x, core).
Axes of the slice: x: 4, y: 4, z: 16, core: 2. Of those that a mesh axis runs over, the one named last changes fastest.
Arguments:
- video: bfloat16 [512, 8, 16, 640], P(('dp', 'frames'), 'height'), parts along dimension 0
- window_gaps: int32 [112], P('dp'), parts along dimension 0, may hold values from 1 to 8, 112 in all
- gn_gain: float32 [640], replicated, may hold values from 0.25 to 1.75
- gn_bias: float32 [640], replicated, may hold values from -3 to 3
- conv_weight: bfloat16 [5760, 640], P('frames', 'height'), may hold values from -0.078125 to 0.078125
- conv_bias: float32 [640], replicated, may hold values from -3 to 3
- ln_gain: float32 [640], replicated, may hold values from 0.25 to 1.75
- ln_bias: float32 [640], replicated, may hold values from -3 to 3
- qkv_weight: bfloat16 [640, 1920], replicated, may hold values from -0.25 to 0.25
- out_weight: bfloat16 [640, 640], replicated, may hold values from -0.5 to 0.5
- out_bias: float32 [640], replicated, may hold values from -3 to 3
Outputs:
- output: bfloat16 [512, 8, 16, 640], P(('dp', 'frames'), 'height'), parts along dimension 0
There are 4 independent parts, one for each index of `dp`. A program takes and returns all parts, laid end to end along the dimension named above; an argument that names none is the same for every part. Nothing has to cross between parts.
Inputs may be any that keep to these rules, and one draw needn't show every extreme that they name: `window_gaps`: the first window starts at frame 0 and the last at 112; the largest gap 16 // 2 is reached in every draw.
All inputs are finite; a program needn't handle non-finite values.
Results may differ from a plain program's by a relative error of at most 0.008.
Values may be sent and summed in bfloat16 or wider, within the bound.
No kernel may reach another device: no remote copies, remote signals or barrier semaphores. Data moves between devices by JAX's collectives and lax.ppermute only.
A program may use at most 64 MiB of HBM per device.

v0:
```python
import jax
import jax.numpy as jnp
from jax import lax
from jax.sharding import PartitionSpec as P

HEADS = 10
GROUPS = 32
WIN = 16
HEAD_DIM = 64
EPSILON = 1e-05


def passed_along(shard, axis, by):
    size = lax.axis_size(axis)
    pairs = [(i, i + by) for i in range(size) if 0 <= i + by < size]
    return lax.ppermute(shard, axis, pairs)


def extended_2(cells, sides, width):
    for axis, dim in sides:
        count = lax.axis_size(axis)
        ends = count - 1
        head = lax.slice_in_dim(cells, 0, width, axis=dim)
        tail = lax.slice_in_dim(cells, cells.shape[dim] - width, cells.shape[dim], axis=dim)
        cells = jnp.concatenate(
            [
                lax.ppermute(tail, axis, [(i, (i + 1) % count) for i in range(ends)]),
                cells,
                lax.ppermute(head, axis, [((i + 1) % count, i) for i in range(ends)]),
            ],
            axis=dim,
        )
    return cells


def fetch_neighbour(keys, values, offset):
    return passed_along((keys, values), "frames", offset)


def window_starts(window_gaps):
    return jnp.concatenate([jnp.zeros((1,), jnp.int32), jnp.cumsum(window_gaps)])


def on_device(
    video,
    window_gaps,
    gn_gain,
    gn_bias,
    conv_weight,
    conv_bias,
    ln_gain,
    ln_bias,
    qkv_weight,
    out_weight,
    out_bias,
):
    frames_dev, rows_dev, width, chans = video.shape
    bands = lax.axis_size("height")
    floats = video.astype(jnp.float32)
    grouped = floats.reshape(frames_dev, rows_dev, width, GROUPS, chans // GROUPS)
    cell_count = rows_dev * bands * width * (chans // GROUPS)
    mean = lax.psum(jnp.sum(grouped, axis=(1, 2, 4)), "height") / cell_count
    centred = grouped - mean[:, None, None, :, None]
    variance = lax.psum(jnp.sum(centred * centred, axis=(1, 2, 4)), "height") / cell_count
    scaled = (grouped - mean[:, None, None, :, None]) * lax.rsqrt(variance + EPSILON)[
        :, None, None, :, None
    ]
    normed = scaled.reshape(floats.shape) * gn_gain + gn_bias
    activated = jax.nn.silu(normed).astype(jnp.bfloat16)
    columns = lax.all_gather(conv_weight, "height", axis=1, tiled=True)
    extended = extended_2(activated, (("height", 1),), 1)
    extended = jnp.pad(extended, ((0, 0), (0, 0), (1, 1), (0, 0)))
    patches = jnp.concatenate(
        [
            extended[:, row_off : row_off + rows_dev, col_off : col_off + width]
            for row_off in range(3)
            for col_off in range(3)
        ],
        axis=3,
    ).reshape(-1, 9 * chans)
    conv_sum = jnp.dot(
        patches,
        lax.all_gather(columns, "frames", axis=0, tiled=True),
        preferred_element_type=jnp.float32,
    )
    conv_out = (
        (conv_sum + conv_bias).astype(jnp.bfloat16).reshape(frames_dev, rows_dev, width, chans)
    )
    conv_out = lax.optimization_barrier(conv_out)
    resid_state = (floats + conv_out.astype(jnp.float32)).astype(jnp.bfloat16)
    resid_float = resid_state.astype(jnp.float32)
    centre = jnp.mean(resid_float, axis=-1, keepdims=True)
    deviation = resid_float - centre
    spread = jnp.mean(deviation * deviation, axis=-1, keepdims=True)
    normalized = (deviation * lax.rsqrt(spread + EPSILON) * ln_gain + ln_bias).astype(jnp.bfloat16)
    cells = rows_dev * width
    project = jnp.dot(
        normalized.reshape(-1, chans), qkv_weight, preferred_element_type=jnp.float32
    ).astype(jnp.bfloat16)
    scale = HEAD_DIM ** (-0.5)
    starts = window_starts(window_gaps)
    project = project.reshape(frames_dev, cells, 3 * chans)
    query = project[:, :, :chans]
    keys = project[:, :, chans : 2 * chans]
    values = project[:, :, 2 * chans :]
    gathered = [fetch_neighbour(keys, values, offset) for offset in (2, 1)]
    gathered.append((keys, values))
    gathered = gathered + [fetch_neighbour(keys, values, offset) for offset in (-1, -2)]
    keys_near = jnp.concatenate([pair[0] for pair in gathered], axis=0).reshape(
        -1, cells, HEADS, HEAD_DIM
    )
    values_near = jnp.concatenate([pair[1] for pair in gathered], axis=0).reshape(
        -1, cells, HEADS, HEAD_DIM
    )
    near_ids = (lax.axis_index("frames") - 2) * frames_dev + jnp.arange(
        5 * frames_dev, dtype=jnp.int32
    )
    inside = (near_ids[None, :] >= starts[:, None]) & (near_ids[None, :] < starts[:, None] + WIN)
    member = inside.astype(jnp.float32)
    cover = member[:, 2 * frames_dev : 3 * frames_dev].T
    frame_count = jnp.sum(cover, axis=1)
    scores = (
        jnp.einsum(
            "nshd,mshd->shnm",
            query.reshape(frames_dev, cells, HEADS, HEAD_DIM),
            keys_near,
            preferred_element_type=jnp.float32,
        )
        * scale
    )
    expo = jnp.exp(scores)
    window_sum = jnp.einsum("shnm,wm->shnw", expo, member, precision=lax.Precision.HIGHEST)
    coef = cover / (frame_count[:, None] * jnp.where(cover > 0, window_sum, 1.0))
    spread_back = jnp.einsum("shnw,wm->shnm", coef, member, precision=lax.Precision.HIGHEST)
    attn_weight = (expo * spread_back).astype(jnp.bfloat16)
    mixed = (
        jnp.einsum("shnm,mshd->nshd", attn_weight, values_near, preferred_element_type=jnp.float32)
        .astype(jnp.bfloat16)
        .reshape(-1, chans)
    )
    projected = jnp.dot(mixed, out_weight, preferred_element_type=jnp.float32)
    output = resid_float.reshape(-1, chans) + projected + out_bias
    return output.astype(jnp.bfloat16).reshape(frames_dev, rows_dev, width, chans)


def solution(mesh):
    placed = (
        P(("dp", "frames"), "height", None, None),
        P("dp"),
        P(),
        P(),
        P("frames", "height"),
        P(),
        P(),
        P(),
        P(),
        P(),
        P(),
    )
    return jax.shard_map(
        on_device,
        mesh=mesh,
        in_specs=placed,
        out_specs=P(("dp", "frames"), "height", None, None),
        check_vma=False,
    )
```

profile of v0, /device:TPU:2, one launch (start us, length us, event | category | flops | bytes accessed | tf_op | source)
XLA Modules:
  0.0 188.5 jit_solution(935710017307930549)
XLA Ops:
  6.5 16.2 %all_gather.6 = bf16[360,640]{0,1:T(8,128)(2,1)S(1)} all-gather(bf16[360,80]{0,1:T(8,128)(2,1)} %param.15), channel_id=1, replica_groups=mesh['dp'=4,'frames'=16,'height'=8] {'height'}, dimensions={1}, use_global_device_ids=true | all-gather | bytes 518400 | tf_op jit(solution)/shard_map/all_gather | solution.py:70
  22.7 1.0 copy.46
  24.2 13.0 %psum.14 = f32[8,32]{1,0:T(8,128)S(1)} all-reduce(f32[8,32]{1,0:T(8,128)S(1)} %reduce_sum.61), channel_id=1, replica_groups=mesh['dp'=4,'frames'=16,'height'=8] {'height'}, use_global_device_ids=true, to_apply=%region_2.0 | all-reduce | flops 256 | bytes 2048 | tf_op jit(solution)/shard_map/psum | solution.py:62
  37.8 12.3 %psum.15 = f32[8,32]{1,0:T(8,128)S(1)} all-reduce(f32[8,32]{1,0:T(8,128)S(1)} %reduce_sum.64), channel_id=1, replica_groups=mesh['dp'=4,'frames'=16,'height'=8] {'height'}, use_global_device_ids=true, to_apply=%region_5.6 | all-reduce | flops 256 | bytes 2048 | tf_op jit(solution)/shard_map/psum | solution.py:64
  50.5 1.9 %collective-permute-start = (bf16[8,1,16,640]{3,2,1,0:T(8,128)(2,1)S(1)}, bf16[8,1,16,640]{3,2,1,0:T(8,128)(2,1)S(1)}, u32[]{:S(2)}, u32[]{:S(2)}) collective-permute-start(bf16[8,1,16,640]{3,2,1,0:T(8,128)(2,1)S(1)} %fusion.38), channel_id=1, source_target_pairs={{0,1},{1,2},{2,3},{3,4},{4,5},{5,6},{6,7},{8,9},{9,10},{10,11},{11... | collective-permute-start | bytes 491528 | tf_op jit(solution)/shard_map/ppermute | solution.py:27
  52.4 4.7 %collective-permute-start.1 = (bf16[8,1,16,640]{3,2,1,0:T(8,128)(2,1)S(1)}, bf16[8,1,16,640]{3,2,1,0:T(8,128)(2,1)S(1)}, u32[]{:S(2)}, u32[]{:S(2)}) collective-permute-start(bf16[8,1,16,640]{3,2,1,0:T(8,128)(2,1)S(1)} %fusion.38), channel_id=1, source_target_pairs={{1,0},{2,1},{3,2},{4,3},{5,4},{6,5},{7,6},{9,8},{10,9},{11,10},{12... | collective-permute-start | bytes 491528 | tf_op jit(solution)/shard_map/ppermute | solution.py:29
  58.2 1.8 collective-permute-done.1
  61.6 0.7 slice_dynamic-update-slice_fusion.4
  63.1 0.8 constant_dynamic-update-slice_fusion.1
  63.9 0.8 slice_dynamic-update-slice_fusion.2
  66.0 0.8 slice_dynamic-update-slice_fusion
  66.7 54.3 %all-gather.2.cloned.1.call-done = bf16[5760,640]{1,0:T(8,128)(2,1)} async-done(((bf16[360,640]{1,0:T(8,128)(2,1)}), bf16[5760,640]{1,0:T(8,128)(2,1)}) %all-gather.2.cloned.1.call-update) | async-done | bytes 7372816 | tf_op jit(solution)/shard_map/all_gather | solution.py:83
  121.0 4.9 %fusion.21 = bf16[128,640]{1,0:T(8,128)(2,1)S(1)} fusion(bf16[128,5760]{1,0:T(8,128)(2,1)} %bitcast, bf16[5760,640]{1,0:T(8,128)(2,1)} %all-gather.2.cloned.1.call-done, f32[640]{0:T(1024)S(1)} %copy-done.6), kind=kOutput, calls=%fused_computation.20 | convolution fusion | flops 943882240 | bytes 9013760 | tf_op jit(solution)/shard_map/dot_general | solution.py:81
  127.1 2.7 %collective-permute-start.6 = (bf16[8,16,640]{2,1,0:T(8,128)(2,1)S(1)}, bf16[8,16,640]{2,1,0:T(8,128)(2,1)S(1)}, u32[]{:S(2)}, u32[]{:S(2)}) collective-permute-start(bf16[8,16,640]{2,1,0:T(8,128)(2,1)S(1)} %get-tuple-element.11), channel_id=1, source_target_pairs={{0,16},{8,24},{16,32},{24,40},{32,48},{40,56},{48,64},{56,72},{64,... | collective-permute-start | bytes 491528 | tf_op jit(solution)/shard_map/ppermute | solution.py:16
  129.8 4.9 %collective-permute-start.2 = (bf16[8,16,640]{2,1,0:T(8,128)(2,1)S(1)}, bf16[8,16,640]{2,1,0:T(8,128)(2,1)S(1)}, u32[]{:S(2)}, u32[]{:S(2)}) collective-permute-start(bf16[8,16,640]{2,1,0:T(8,128)(2,1)S(1)} %get-tuple-element.10), channel_id=1, source_target_pairs={{0,16},{8,24},{16,32},{24,40},{32,48},{40,56},{48,64},{56,72},{64,... | collective-permute-start | bytes 491528 | tf_op jit(solution)/shard_map/ppermute | solution.py:16
  134.8 3.8 %collective-permute-start.7 = (bf16[8,16,640]{2,1,0:T(8,128)(2,1)S(1)}, bf16[8,16,640]{2,1,0:T(8,128)(2,1)S(1)}, u32[]{:S(2)}, u32[]{:S(2)}) collective-permute-start(bf16[8,16,640]{2,1,0:T(8,128)(2,1)S(1)} %get-tuple-element.11), channel_id=1, source_target_pairs={{0,8},{8,16},{16,24},{24,32},{32,40},{40,48},{48,56},{56,64},{64,7... | collective-permute-start | bytes 491528 | tf_op jit(solution)/shard_map/ppermute | solution.py:16
  138.6 3.8 %collective-permute-start.3 = (bf16[8,16,640]{2,1,0:T(8,128)(2,1)S(1)}, bf16[8,16,640]{2,1,0:T(8,128)(2,1)S(1)}, u32[]{:S(2)}, u32[]{:S(2)}) collective-permute-start(bf16[8,16,640]{2,1,0:T(8,128)(2,1)S(1)} %get-tuple-element.10), channel_id=1, source_target_pairs={{0,8},{8,16},{16,24},{24,32},{32,40},{40,48},{48,56},{56,64},{64,7... | collective-permute-start | bytes 491528 | tf_op jit(solution)/shard_map/ppermute | solution.py:16
  142.4 1.3 collective-permute-start.4
  143.7 1.3 collective-permute-start.5
  145.0 1.3 collective-permute-start.8
  147.0 1.3 collective-permute-start.9
  149.0 0.7 constant_dynamic-update-slice_fusion.5
  149.7 0.9 copy-done.3
  150.6 0.9 collective-permute-done.4
  152.2 7.9 %collective-permute-done.5 = bf16[8,16,640]{2,1,0:T(8,128)(2,1)S(1)} collective-permute-done((bf16[8,16,640]{2,1,0:T(8,128)(2,1)S(1)}, bf16[8,16,640]{2,1,0:T(8,128)(2,1)S(1)}, u32[]{:S(2)}, u32[]{:S(2)}) %collective-permute-start.5) | collective-permute-done | bytes 163872 | tf_op jit(solution)/shard_map/ppermute | solution.py:16
  160.8 4.1 %reshape.144 = bf16[40,16,10,64]{3,2,1,0:T(8,128)(2,1)} reshape(bf16[40,16,640]{2,1,0:T(8,128)(2,1)} %constant_dynamic-update-slice_fusion.3) | data formatting | bytes 1638400 | tf_op jit(solution)/shard_map/reshape | solution.py:112
  165.6 2.7 %collective-permute-done.9 = bf16[8,16,640]{2,1,0:T(8,128)(2,1)S(1)} collective-permute-done((bf16[8,16,640]{2,1,0:T(8,128)(2,1)S(1)}, bf16[8,16,640]{2,1,0:T(8,128)(2,1)S(1)}, u32[]{:S(2)}, u32[]{:S(2)}) %collective-permute-start.9) | collective-permute-done | bytes 163872 | tf_op jit(solution)/shard_map/ppermute | solution.py:16
  168.9 4.1 %reshape.146 = bf16[40,16,10,64]{3,2,1,0:T(8,128)(2,1)} reshape(bf16[40,16,640]{2,1,0:T(8,128)(2,1)} %constant_dynamic-update-slice_fusion.8) | data formatting | bytes 1638400 | tf_op jit(solution)/shard_map/reshape | solution.py:109
  173.3 3.0 %fusion.8 = f32[16,10,8,40]{3,2,1,0:T(8,128)S(1)} fusion(bf16[40,16,10,64]{3,2,1,0:T(8,128)(2,1)} %reshape.146, bf16[8,16,10,64]{3,2,1,0:T(8,128)(2,1)S(1)} %reshape.145), kind=kOutput, calls=%fused_computation.10 | convolution fusion | flops 6604800 | bytes 1187840 | tf_op jit(solution)/shard_map/nshd,mshd->shnm/dot_general | solution.py:123
  177.3 0.7 copy-done.2
  178.0 1.0 fusion.18
  179.5 2.1 %fusion.22 = bf16[128,640]{1,0:T(8,128)(2,1)} fusion(bf16[128,640]{1,0:T(8,128)(2,1)S(1)} %reshape.149, bf16[640,640]{1,0:T(8,128)(2,1)} %param.20, f32[640]{0:T(1024)S(1)} %copy-done.9, bf16[128,640]{1,0:T(8,128)(2,1)S(1)} %bitcast.36), kind=kOutput, calls=%fused_computation.21 | convolution fusion | flops 105185280 | bytes 1313280 | tf_op jit(solution)/shard_map/dot_general | solution.py:141
  (76 shorter events, 13.0 us)
Async XLA Ops:
  6.5 119.9 %copy-start = (bf16[640,1920]{1,0:T(8,128)(2,1)S(1)}, bf16[640,1920]{1,0:T(8,128)(2,1)}, u32[]{:S(2)}) copy-start(bf16[640,1920]{1,0:T(8,128)(2,1)} %param.19) | copy-start | bytes 7372804
  6.5 17.3 %copy-start.1 = (bf16[8,1,16,640]{3,2,1,0:T(8,128)(2,1)S(1)}, bf16[8,1,16,640]{3,2,1,0:T(8,128)(2,1)}, u32[]{:S(2)}) copy-start(bf16[8,1,16,640]{3,2,1,0:T(8,128)(2,1)} %param.11) | copy-start | bytes 491524
  6.5 114.5 %all-gather.2.cloned.1.call-start = ((), (), s32[]{:S(2)}) async-start(), calls=%async_computation | async-start | bytes 7833600 | tf_op jit(solution)/shard_map/all_gather | solution.py:83
  22.7 27.6 %copy-start.4 = (f32[640]{0:T(1024)S(1)}, f32[640]{0:T(1024)}, u32[]{:S(2)}) copy-start(f32[640]{0:T(1024)} %param.14) | copy-start | bytes 7684
  22.7 27.6 %copy-start.5 = (f32[640]{0:T(1024)S(1)}, f32[640]{0:T(1024)}, u32[]{:S(2)}) copy-start(f32[640]{0:T(1024)} %param.13) | copy-start | bytes 7684
  22.7 34.4 %copy-start.10 = (s32[28]{0:T(128)S(1)}, s32[28]{0:T(128)}, u32[]{:S(2)}) copy-start(s32[28]{0:T(128)} %param.12) | copy-start | bytes 340
  50.5 7.7 %collective-permute-start = (bf16[8,1,16,640]{3,2,1,0:T(8,128)(2,1)S(1)}, bf16[8,1,16,640]{3,2,1,0:T(8,128)(2,1)S(1)}, u32[]{:S(2)}, u32[]{:S(2)}) collective-permute-start(bf16[8,1,16,640]{3,2,1,0:T(8,128)(2,1)S(1)} %fusion.38), channel_id=1, source_target_pairs={{0,1},{1,2},{2,3},{3,4},{4,5},{5,6},{6,7},{8,9},{9,10},{10,11},{11... | collective-permute-start | bytes 491528 | tf_op jit(solution)/shard_map/ppermute | solution.py:27
  52.4 7.5 %collective-permute-start.1 = (bf16[8,1,16,640]{3,2,1,0:T(8,128)(2,1)S(1)}, bf16[8,1,16,640]{3,2,1,0:T(8,128)(2,1)S(1)}, u32[]{:S(2)}, u32[]{:S(2)}) collective-permute-start(bf16[8,1,16,640]{3,2,1,0:T(8,128)(2,1)S(1)} %fusion.38), channel_id=1, source_target_pairs={{1,0},{2,1},{3,2},{4,3},{5,4},{6,5},{7,6},{9,8},{10,9},{11,10},{12... | collective-permute-start | bytes 491528 | tf_op jit(solution)/shard_map/ppermute | solution.py:29
  60.2 60.8 %copy-start.6 = (f32[640]{0:T(1024)S(1)}, f32[640]{0:T(1024)}, u32[]{:S(2)}) copy-start(f32[640]{0:T(1024)} %param.16) | copy-start | bytes 7684
  121.0 5.3 %copy-start.7 = (f32[640]{0:T(1024)S(1)}, f32[640]{0:T(1024)}, u32[]{:S(2)}) copy-start(f32[640]{0:T(1024)} %param.18) | copy-start | bytes 7684
  121.0 5.3 %copy-start.8 = (f32[640]{0:T(1024)S(1)}, f32[640]{0:T(1024)}, u32[]{:S(2)}) copy-start(f32[640]{0:T(1024)} %param.17) | copy-start | bytes 7684
  127.1 16.6 %collective-permute-start.6 = (bf16[8,16,640]{2,1,0:T(8,128)(2,1)S(1)}, bf16[8,16,640]{2,1,0:T(8,128)(2,1)S(1)}, u32[]{:S(2)}, u32[]{:S(2)}) collective-permute-start(bf16[8,16,640]{2,1,0:T(8,128)(2,1)S(1)} %get-tuple-element.11), channel_id=1, source_target_pairs={{0,16},{8,24},{16,32},{24,40},{32,48},{40,56},{48,64},{56,72},{64,... | collective-permute-start | bytes 491528 | tf_op jit(solution)/shard_map/ppermute | solution.py:16
  129.8 15.2 %collective-permute-start.2 = (bf16[8,16,640]{2,1,0:T(8,128)(2,1)S(1)}, bf16[8,16,640]{2,1,0:T(8,128)(2,1)S(1)}, u32[]{:S(2)}, u32[]{:S(2)}) collective-permute-start(bf16[8,16,640]{2,1,0:T(8,128)(2,1)S(1)} %get-tuple-element.10), channel_id=1, source_target_pairs={{0,16},{8,24},{16,32},{24,40},{32,48},{40,56},{48,64},{56,72},{64,... | collective-permute-start | bytes 491528 | tf_op jit(solution)/shard_map/ppermute | solution.py:16
  134.8 12.2 %collective-permute-start.7 = (bf16[8,16,640]{2,1,0:T(8,128)(2,1)S(1)}, bf16[8,16,640]{2,1,0:T(8,128)(2,1)S(1)}, u32[]{:S(2)}, u32[]{:S(2)}) collective-permute-start(bf16[8,16,640]{2,1,0:T(8,128)(2,1)S(1)} %get-tuple-element.11), channel_id=1, source_target_pairs={{0,8},{8,16},{16,24},{24,32},{32,40},{40,48},{48,56},{56,64},{64,7... | collective-permute-start | bytes 491528 | tf_op jit(solution)/shard_map/ppermute | solution.py:16
  138.6 9.7 %collective-permute-start.3 = (bf16[8,16,640]{2,1,0:T(8,128)(2,1)S(1)}, bf16[8,16,640]{2,1,0:T(8,128)(2,1)S(1)}, u32[]{:S(2)}, u32[]{:S(2)}) collective-permute-start(bf16[8,16,640]{2,1,0:T(8,128)(2,1)S(1)} %get-tuple-element.10), channel_id=1, source_target_pairs={{0,8},{8,16},{16,24},{24,32},{32,40},{40,48},{48,56},{56,64},{64,7... | collective-permute-start | bytes 491528 | tf_op jit(solution)/shard_map/ppermute | solution.py:16
  142.4 9.1 %collective-permute-start.4 = (bf16[8,16,640]{2,1,0:T(8,128)(2,1)S(1)}, bf16[8,16,640]{2,1,0:T(8,128)(2,1)S(1)}, u32[]{:S(2)}, u32[]{:S(2)}) collective-permute-start(bf16[8,16,640]{2,1,0:T(8,128)(2,1)S(1)} %get-tuple-element.10), channel_id=1, source_target_pairs={{8,0},{16,8},{24,16},{32,24},{40,32},{48,40},{56,48},{64,56},{72,6... | collective-permute-start | bytes 491528 | tf_op jit(solution)/shard_map/ppermute | solution.py:16
  143.7 16.5 %collective-permute-start.5 = (bf16[8,16,640]{2,1,0:T(8,128)(2,1)S(1)}, bf16[8,16,640]{2,1,0:T(8,128)(2,1)S(1)}, u32[]{:S(2)}, u32[]{:S(2)}) collective-permute-start(bf16[8,16,640]{2,1,0:T(8,128)(2,1)S(1)} %get-tuple-element.10), channel_id=1, source_target_pairs={{16,0},{24,8},{32,16},{40,24},{48,32},{56,40},{64,48},{72,56},{80,... | collective-permute-start | bytes 491528 | tf_op jit(solution)/shard_map/ppermute | solution.py:16
  145.0 19.9 %collective-permute-start.8 = (bf16[8,16,640]{2,1,0:T(8,128)(2,1)S(1)}, bf16[8,16,640]{2,1,0:T(8,128)(2,1)S(1)}, u32[]{:S(2)}, u32[]{:S(2)}) collective-permute-start(bf16[8,16,640]{2,1,0:T(8,128)(2,1)S(1)} %get-tuple-element.11), channel_id=1, source_target_pairs={{8,0},{16,8},{24,16},{32,24},{40,32},{48,40},{56,48},{64,56},{72,6... | collective-permute-start | bytes 491528 | tf_op jit(solution)/shard_map/ppermute | solution.py:16
  147.0 21.3 %collective-permute-start.9 = (bf16[8,16,640]{2,1,0:T(8,128)(2,1)S(1)}, bf16[8,16,640]{2,1,0:T(8,128)(2,1)S(1)}, u32[]{:S(2)}, u32[]{:S(2)}) collective-permute-start(bf16[8,16,640]{2,1,0:T(8,128)(2,1)S(1)} %get-tuple-element.11), channel_id=1, source_target_pairs={{16,0},{24,8},{32,16},{40,24},{48,32},{56,40},{64,48},{72,56},{80,... | collective-permute-start | bytes 491528 | tf_op jit(solution)/shard_map/ppermute | solution.py:16
  149.7 0.9 copy-start.3
  176.3 1.8 copy-start.2
  178.0 1.5 copy-start.9
Sparse Core Ops, SparseCore 0:
  23.9 97.0 all-gather.1
where the time goes:
time: 189 us; the launch traced here: 188 us
  waiting for transfers between devices  68.2 us (36%)
  blocking collectives  41.6 us (22%)
  starting transfers between devices  26.9 us (14%)
  local copies, waits for them, and re-layouts  23 us (12%)
  between operations  13.8 us (7%)
  matrix products  12.6 us (7%)
  other arithmetic  2.48 us (1%)
    all_gather x1, waiting for transfers between devices, on_device(): lax.all_gather(columns, 'frames', axis=0, tiled=True)  54.3 us
    ppermute x8, starting transfers between devices, passed_along(): return lax.ppermute(shard, axis, pairs)  20.3 us
    all_gather x1, blocking collectives, on_device(): columns = lax.all_gather(conv_weight, 'height', axis=1, tiled=True)  16.2 us
    psum x1, blocking collectives, on_device(): mean = lax.psum(jnp.sum(grouped, axis=(1, 2, 4)), 'height') / cell_count  13 us
    psum x1, blocking collectives, on_device(): lax.psum(jnp.sum(centred * centred, axis=(1, 2, 4)), 'height') / cell_count  12.3 us
    ppermute x8, waiting for transfers between devices, passed_along(): return lax.ppermute(shard, axis, pairs)  11.5 us
    unnamed x36, local copies, waits for them, and re-layouts  10.1 us
    dot_general x1, matrix products, on_device(): jnp.dot(patches, lax.all_gather(columns, 'frames', axis=0, tiled=True), p...  4.9 us
  transfers between devices with their start and end apart: 11, of which 6 were waited for; matrix products, arithmetic and copies ran while one was open for 9% of the time, Pallas kernels for 0%

commit v1 on v0

--- a/solution.py
+++ b/solution.py
@@ -80,7 +80,9 @@
     ).reshape(-1, 9 * chans)
     conv_sum = jnp.dot(
         patches,
-        lax.all_gather(columns, "frames", axis=0, tiled=True),
+        jnp.concatenate(
+            lax.all_to_all(jnp.stack([columns] * lax.axis_size("frames")), "frames", 0, 0), axis=0
+        ),
         preferred_element_type=jnp.float32,
     )
     conv_out = (

time: 189 us -> 416 us (2.20)
  the two profiles are of different devices: /device:TPU:2 before, /device:TPU:16 now
where the time goes in v1:
time: 416 us; the launch traced here: 415 us
  waiting for transfers between devices  290 us (70%)
  blocking collectives  41.9 us (10%)
  starting transfers between devices  39.9 us (10%)
  local copies, waits for them, and re-layouts  27.5 us (7%)
  matrix products  12.6 us (3%)
    all_to_all x1, waiting for transfers between devices, on_device(): lax.all_to_all(jnp.stack([columns] * lax.axis_size('frames')), 'frames',...  278 us
    ppermute x8, starting transfers between devices, passed_along(): return lax.ppermute(shard, axis, pairs)  21.8 us
    all_to_all x1, starting transfers between devices, on_device(): lax.all_to_all(jnp.stack([columns] * lax.axis_size('frames')), 'frames',...  15.4 us
    psum x1, blocking collectives, on_device(): mean = lax.psum(jnp.sum(grouped, axis=(1, 2, 4)), 'height') / cell_count  14.9 us
    all_gather x1, blocking collectives, on_device(): columns = lax.all_gather(conv_weight, 'height', axis=1, tiled=True)  13.8 us
    psum x1, blocking collectives, on_device(): lax.psum(jnp.sum(centred * centred, axis=(1, 2, 4)), 'height') / cell_count  13.2 us
    unnamed x38, local copies, waits for them, and re-layouts  11.3 us
    ppermute x8, waiting for transfers between devices, passed_along(): return lax.ppermute(shard, axis, pairs)  10.8 us
  transfers between devices with their start and end apart: 11, of which 4 were waited for; matrix products, arithmetic and copies ran while one was open for 4% of the time, Pallas kernels for 0%

profile of v1, /device:TPU:16, one launch (start us, length us, event | category | flops | bytes accessed | tf_op | source)
XLA Modules:
  0.0 415.2 jit_solution(3413460457292602808)
XLA Ops:
  0.0 13.8 %all_gather.3 = bf16[360,640]{0,1:T(8,128)(2,1)S(1)} all-gather(bf16[360,80]{0,1:T(8,128)(2,1)} %param.15), channel_id=1, replica_groups=mesh['dp'=4,'frames'=16,'height'=8] {'height'}, dimensions={1}, use_global_device_ids=true | all-gather | bytes 518400 | tf_op jit(solution)/shard_map/all_gather | solution.py:70
  14.0 3.6 stack.2
  17.6 15.4 %all-to-all-start = ((bf16[16,360,640]{2,1,0:T(8,128)(2,1)}), bf16[16,360,640]{2,1,0:T(8,128)(2,1)}, u32[]{:S(2)}, u32[]{:S(2)}) async-start(bf16[16,360,640]{2,1,0:T(8,128)(2,1)} %stack.2), calls=%async_computation | async-start | bytes 14745600 | tf_op jit(solution)/shard_map/all_to_all | solution.py:84
  33.3 14.9 %psum.14 = f32[8,32]{1,0:T(8,128)S(1)} all-reduce(f32[8,32]{1,0:T(8,128)S(1)} %reduce_sum.61), channel_id=1, replica_groups=mesh['dp'=4,'frames'=16,'height'=8] {'height'}, use_global_device_ids=true, to_apply=%region_2.0 | all-reduce | flops 256 | bytes 2048 | tf_op jit(solution)/shard_map/psum | solution.py:62
  48.8 13.2 %psum.15 = f32[8,32]{1,0:T(8,128)S(1)} all-reduce(f32[8,32]{1,0:T(8,128)S(1)} %reduce_sum.64), channel_id=1, replica_groups=mesh['dp'=4,'frames'=16,'height'=8] {'height'}, use_global_device_ids=true, to_apply=%region_5.6 | all-reduce | flops 256 | bytes 2048 | tf_op jit(solution)/shard_map/psum | solution.py:64
  62.4 1.4 collective-permute-start
  63.8 1.3 collective-permute-start.1
  65.7 1.5 collective-permute-done.1
  70.2 0.8 constant_dynamic-update-slice_fusion.1
  74.0 278.1 %all-to-all-done = bf16[16,360,640]{2,1,0:T(8,128)(2,1)} async-done(((bf16[16,360,640]{2,1,0:T(8,128)(2,1)}), bf16[16,360,640]{2,1,0:T(8,128)(2,1)}, u32[]{:S(2)}, u32[]{:S(2)}) %all-to-all-start) | async-done | bytes 7372832 | tf_op jit(solution)/shard_map/all_to_all | solution.py:84
  352.1 4.9 %fusion.21 = bf16[128,640]{1,0:T(8,128)(2,1)S(1)} fusion(bf16[128,5760]{1,0:T(8,128)(2,1)} %bitcast, bf16[5760,640]{1,0:T(8,128)(2,1)} %bitcast.1, f32[640]{0:T(1024)S(1)} %copy-done.7), kind=kOutput, calls=%fused_computation.20 | convolution fusion | flops 943882240 | bytes 9013760 | tf_op jit(solution)/shard_map/dot_general | solution.py:81
  358.8 5.1 %collective-permute-start.6 = (bf16[8,16,640]{2,1,0:T(8,128)(2,1)}, bf16[8,16,640]{2,1,0:T(8,128)(2,1)}, u32[]{:S(2)}, u32[]{:S(2)}) collective-permute-start(bf16[8,16,640]{2,1,0:T(8,128)(2,1)} %get-tuple-element.11), channel_id=1, source_target_pairs={{0,16},{8,24},{16,32},{24,40},{32,48},{40,56},{48,64},{56,72},{64,... | collective-permute-start | bytes 491528 | tf_op jit(solution)/shard_map/ppermute | solution.py:16
  364.0 4.5 %collective-permute-start.2 = (bf16[8,16,640]{2,1,0:T(8,128)(2,1)S(1)}, bf16[8,16,640]{2,1,0:T(8,128)(2,1)S(1)}, u32[]{:S(2)}, u32[]{:S(2)}) collective-permute-start(bf16[8,16,640]{2,1,0:T(8,128)(2,1)S(1)} %get-tuple-element.10), channel_id=1, source_target_pairs={{0,16},{8,24},{16,32},{24,40},{32,48},{40,56},{48,64},{56,72},{64,... | collective-permute-start | bytes 491528 | tf_op jit(solution)/shard_map/ppermute | solution.py:16
  368.7 3.5 collective-permute-start.7
  372.3 3.3 collective-permute-start.3
  375.6 1.3 collective-permute-start.4
  376.9 1.3 collective-permute-start.5
  378.2 0.9 constant_dynamic-update-slice_fusion.12
  379.2 1.3 collective-permute-start.8
  381.2 1.5 collective-permute-start.9
  383.3 0.8 constant_dynamic-update-slice_fusion.5
  384.1 0.9 copy-done.3
  385.7 7.7 %collective-permute-done.5 = bf16[8,16,640]{2,1,0:T(8,128)(2,1)S(1)} collective-permute-done((bf16[8,16,640]{2,1,0:T(8,128)(2,1)S(1)}, bf16[8,16,640]{2,1,0:T(8,128)(2,1)S(1)}, u32[]{:S(2)}, u32[]{:S(2)}) %collective-permute-start.5) | collective-permute-done | bytes 163872 | tf_op jit(solution)/shard_map/ppermute | solution.py:16
  394.1 4.2 reshape.150
  398.3 0.9 constant_dynamic-update-slice_fusion.9
  399.2 3.0 collective-permute-done.9
  402.2 0.9 constant_dynamic-update-slice_fusion.8
  403.1 2.5 reshape.152
  405.7 1.2 reshape.151
  406.9 3.0 fusion.10
  411.6 1.0 fusion.18
  413.1 2.1 fusion.22
  (80 shorter events, 14.9 us)
Async XLA Ops:
  0.0 357.5 %copy-start = (bf16[640,1920]{1,0:T(8,128)(2,1)S(1)}, bf16[640,1920]{1,0:T(8,128)(2,1)}, u32[]{:S(2)}) copy-start(bf16[640,1920]{1,0:T(8,128)(2,1)} %param.19) | copy-start | bytes 7372804
  17.6 15.4 %copy-start.1 = (bf16[8,1,16,640]{3,2,1,0:T(8,128)(2,1)S(1)}, bf16[8,1,16,640]{3,2,1,0:T(8,128)(2,1)}, u32[]{:S(2)}) copy-start(bf16[8,1,16,640]{3,2,1,0:T(8,128)(2,1)} %param.11) | copy-start | bytes 491524
  17.6 334.5 %all-to-all-start = ((bf16[16,360,640]{2,1,0:T(8,128)(2,1)}), bf16[16,360,640]{2,1,0:T(8,128)(2,1)}, u32[]{:S(2)}, u32[]{:S(2)}) async-start(bf16[16,360,640]{2,1,0:T(8,128)(2,1)} %stack.2), calls=%async_computation | async-start | bytes 14745600 | tf_op jit(solution)/shard_map/all_to_all | solution.py:84
  33.0 29.3 %copy-start.5 = (f32[640]{0:T(1024)S(1)}, f32[640]{0:T(1024)}, u32[]{:S(2)}) copy-start(f32[640]{0:T(1024)} %param.14) | copy-start | bytes 7684
  33.0 29.3 %copy-start.6 = (f32[640]{0:T(1024)S(1)}, f32[640]{0:T(1024)}, u32[]{:S(2)}) copy-start(f32[640]{0:T(1024)} %param.13) | copy-start | bytes 7684
  33.0 32.1 %copy-start.11 = (s32[28]{0:T(128)S(1)}, s32[28]{0:T(128)}, u32[]{:S(2)}) copy-start(s32[28]{0:T(128)} %param.12) | copy-start | bytes 340
  62.4 3.2 collective-permute-start
  63.8 3.3 collective-permute-start.1
  67.4 284.7 %copy-start.7 = (f32[640]{0:T(1024)S(1)}, f32[640]{0:T(1024)}, u32[]{:S(2)}) copy-start(f32[640]{0:T(1024)} %param.16) | copy-start | bytes 7684
  352.1 5.3 %copy-start.8 = (f32[640]{0:T(1024)S(1)}, f32[640]{0:T(1024)}, u32[]{:S(2)}) copy-start(f32[640]{0:T(1024)} %param.18) | copy-start | bytes 7684
  352.1 5.3 %copy-start.9 = (f32[640]{0:T(1024)S(1)}, f32[640]{0:T(1024)}, u32[]{:S(2)}) copy-start(f32[640]{0:T(1024)} %param.17) | copy-start | bytes 7684
  358.8 18.1 %collective-permute-start.6 = (bf16[8,16,640]{2,1,0:T(8,128)(2,1)}, bf16[8,16,640]{2,1,0:T(8,128)(2,1)}, u32[]{:S(2)}, u32[]{:S(2)}) collective-permute-start(bf16[8,16,640]{2,1,0:T(8,128)(2,1)} %get-tuple-element.11), channel_id=1, source_target_pairs={{0,16},{8,24},{16,32},{24,40},{32,48},{40,56},{48,64},{56,72},{64,... | collective-permute-start | bytes 491528 | tf_op jit(solution)/shard_map/ppermute | solution.py:16
  364.0 15.2 %collective-permute-start.2 = (bf16[8,16,640]{2,1,0:T(8,128)(2,1)S(1)}, bf16[8,16,640]{2,1,0:T(8,128)(2,1)S(1)}, u32[]{:S(2)}, u32[]{:S(2)}) collective-permute-start(bf16[8,16,640]{2,1,0:T(8,128)(2,1)S(1)} %get-tuple-element.10), channel_id=1, source_target_pairs={{0,16},{8,24},{16,32},{24,40},{32,48},{40,56},{48,64},{56,72},{64,... | collective-permute-start | bytes 491528 | tf_op jit(solution)/shard_map/ppermute | solution.py:16
  368.7 12.4 %collective-permute-start.7 = (bf16[8,16,640]{2,1,0:T(8,128)(2,1)}, bf16[8,16,640]{2,1,0:T(8,128)(2,1)S(1)}, u32[]{:S(2)}, u32[]{:S(2)}) collective-permute-start(bf16[8,16,640]{2,1,0:T(8,128)(2,1)} %get-tuple-element.11), channel_id=1, source_target_pairs={{0,8},{8,16},{16,24},{24,32},{32,40},{40,48},{48,56},{56,64},{64,7... | collective-permute-start | bytes 491528 | tf_op jit(solution)/shard_map/ppermute | solution.py:16
  372.3 10.4 %collective-permute-start.3 = (bf16[8,16,640]{2,1,0:T(8,128)(2,1)S(1)}, bf16[8,16,640]{2,1,0:T(8,128)(2,1)S(1)}, u32[]{:S(2)}, u32[]{:S(2)}) collective-permute-start(bf16[8,16,640]{2,1,0:T(8,128)(2,1)S(1)} %get-tuple-element.10), channel_id=1, source_target_pairs={{0,8},{8,16},{16,24},{24,32},{32,40},{40,48},{48,56},{56,64},{64,7... | collective-permute-start | bytes 491528 | tf_op jit(solution)/shard_map/ppermute | solution.py:16
  375.6 9.4 %collective-permute-start.4 = (bf16[8,16,640]{2,1,0:T(8,128)(2,1)S(1)}, bf16[8,16,640]{2,1,0:T(8,128)(2,1)S(1)}, u32[]{:S(2)}, u32[]{:S(2)}) collective-permute-start(bf16[8,16,640]{2,1,0:T(8,128)(2,1)S(1)} %get-tuple-element.10), channel_id=1, source_target_pairs={{8,0},{16,8},{24,16},{32,24},{40,32},{48,40},{56,48},{64,56},{72,6... | collective-permute-start | bytes 491528 | tf_op jit(solution)/shard_map/ppermute | solution.py:16
  376.9 16.5 %collective-permute-start.5 = (bf16[8,16,640]{2,1,0:T(8,128)(2,1)S(1)}, bf16[8,16,640]{2,1,0:T(8,128)(2,1)S(1)}, u32[]{:S(2)}, u32[]{:S(2)}) collective-permute-start(bf16[8,16,640]{2,1,0:T(8,128)(2,1)S(1)} %get-tuple-element.10), channel_id=1, source_target_pairs={{16,0},{24,8},{32,16},{40,24},{48,32},{56,40},{64,48},{72,56},{80,... | collective-permute-start | bytes 491528 | tf_op jit(solution)/shard_map/ppermute | solution.py:16
  379.2 19.1 %collective-permute-start.8 = (bf16[8,16,640]{2,1,0:T(8,128)(2,1)}, bf16[8,16,640]{2,1,0:T(8,128)(2,1)}, u32[]{:S(2)}, u32[]{:S(2)}) collective-permute-start(bf16[8,16,640]{2,1,0:T(8,128)(2,1)} %get-tuple-element.11), channel_id=1, source_target_pairs={{8,0},{16,8},{24,16},{32,24},{40,32},{48,40},{56,48},{64,56},{72,6... | collective-permute-start | bytes 491528 | tf_op jit(solution)/shard_map/ppermute | solution.py:16
  381.2 21.0 %collective-permute-start.9 = (bf16[8,16,640]{2,1,0:T(8,128)(2,1)}, bf16[8,16,640]{2,1,0:T(8,128)(2,1)}, u32[]{:S(2)}, u32[]{:S(2)}) collective-permute-start(bf16[8,16,640]{2,1,0:T(8,128)(2,1)} %get-tuple-element.11), channel_id=1, source_target_pairs={{16,0},{24,8},{32,16},{40,24},{48,32},{56,40},{64,48},{72,56},{80,... | collective-permute-start | bytes 491528 | tf_op jit(solution)/shard_map/ppermute | solution.py:16
  384.1 0.9 copy-start.3
  394.1 4.2 %copy-start.4 = (bf16[40,16,640]{2,1,0:T(8,128)(2,1)S(1)}, bf16[40,16,640]{2,1,0:T(8,128)(2,1)}, u32[]{:S(2)}) copy-start(bf16[40,16,640]{2,1,0:T(8,128)(2,1)} %copy-done.3) | copy-start | bytes 2457604
  409.9 1.8 copy-start.2
  411.6 1.5 copy-start.10
